TPU v7x, 256 devices: a whole 4x4x8 slice. The times are simulated.
256 devices in a mesh: mem: 4 (over y_hi, core), reg: 64 (over y_lo, x, z).
Axes of the slice: x: 4, y: 4 (y_hi: 2, y_lo: 2; y = y_hi * 2 + y_lo), z: 8, core: 2. Of those that a mesh axis runs over, the one named last changes fastest.
Arguments:
- prior_samples: bfloat16 [256, 512, 512], P('mem', 'reg'), may hold values from -6 to 6
- measured_sample_anomalies: bfloat16 [16384, 128, 256], P(('mem', 'reg')), may hold values from -4 to 4
- reciprocal_noise_spread: float32 [16384, 128], P(('mem', 'reg')), may hold values from 0.3 to 3
- measured_departure: float32 [16384, 128], P(('mem', 'reg')), may hold values from -6 to 6
- measurement_tally: int32 [16384], P(('mem', 'reg')), may hold values from 32 to 128
- group_destination_zone: int32 [16384, 1], P(('mem', 'reg')), may hold values from 0 to 63; in each aligned block of 64 rows (0 to 63, 64 to 127, ...) at most 2 rows name the same one
- group_nearby_tile: int32 [16384], P(('mem', 'reg')), may hold values from 0 to 7
Outputs:
- analysis: bfloat16 [256, 512, 512], P('mem', 'reg')
Inputs may be any that keep to these rules, and one draw needn't show every extreme that they name: `measurement_tally`: valid observations of a block stand in its first rows. `group_destination_zone`: at most 2 of the blocks of one device name the same region; in every draw some device has exactly 2 blocks naming one region.
All inputs are finite; a program needn't handle non-finite values.
Results may differ from a plain program's by a relative error of at most 0.0069.
Values may be sent and summed in bfloat16 or wider, within the bound.
No kernel may reach another device: no remote copies, remote signals or barrier semaphores. Data moves between devices by JAX's collectives and lax.ppermute only.
A program may use at most 128 MiB of HBM per device.

v0:
```python
import functools
import math

import jax
import jax.numpy as jnp
from jax import lax
from jax.experimental import pallas as pl
from jax.experimental.pallas import tpu as pltpu
from jax.sharding import Mesh
from jax.sharding import PartitionSpec as P


SAMPLE_NUMBER = 256
OB = 128
CAP = 2
PATCH_REG = 8
ITERS = 5
META = 8
ROWS = CAP * OB + META
HALF = SAMPLE_NUMBER // 2
MEMBERS = SAMPLE_NUMBER // 4
PACK = 2 * HALF + 16
GROUP = ("mem", "ylo", "x", "zp")
STEP = 8
ALONG = (0, 2, 1, 3)
TAGS = 16


def prep_kernel(
    ways, zone_smem, tally_smem, tile_smem, anom_ref, spread_ref, depart_ref, out_ref, anom_buf,
    meta_wide, counts, sems
):
    blocks = anom_ref.shape[0]
    regions = out_ref.shape[0]
    zq_ways, plane_ways, zp_ways = ways
    zq = lax.axis_index("zq")

    def load(g):
        part = pl.ds(g * STEP, STEP)
        return pltpu.make_async_copy(anom_ref.at[part], anom_buf.at[part], sems.at[g])

    for g in range(blocks // STEP):
        load(g).start()

    @pl.loop(0, regions)
    def _(r):
        counts[r] = 0

    meta_wide[...] = jnp.zeros_like(meta_wide)
    block_row = lax.broadcasted_iota(jnp.int32, (STEP, OB), 0)
    lane = lax.broadcasted_iota(jnp.int32, (STEP, OB), 1)

    @pl.loop(0, blocks // STEP)
    def _(g):
        part = pl.ds(pl.multiple_of(g * STEP, STEP), STEP)
        tally = jnp.zeros((STEP, OB), jnp.int32)
        for j in range(STEP):
            tally = jnp.where(block_row == j, tally_smem[g * STEP + j], tally)
        kept = jnp.where(lane < tally, spread_ref[part, :], 0.0)
        weighted = depart_ref[part, :] * kept
        weight_t = kept.T
        load(g).wait()
        for j in range(STEP):
            b = g * STEP + j
            region = zone_smem[b]
            rank = counts[region]
            counts[region] = rank + 1
            rest = region // zp_ways
            along = (rest % zq_ways - zq + zq_ways) % zq_ways
            mem = along % 2 * 2 + along // 2
            place = (mem * plane_ways + rest // zq_ways) * zp_ways + region % zp_ways

            scaled = anom_buf[b].astype(jnp.float32) * weight_t[:, j : j + 1]
            start = pl.multiple_of(rank * OB, OB)
            out_ref[place, pl.ds(start, OB), :] = scaled.astype(jnp.bfloat16)

            tag = jnp.full((1, OB), tile_smem[b] + 1, jnp.int32).astype(jnp.float32)
            content = jnp.concatenate([weighted[j : j + 1], tag], axis=1)
            meta_wide[place, pl.ds(rank, 1), :] = content

    out_ref[:, CAP * OB :, :] = meta_wide[...].astype(jnp.bfloat16)


def build_messages(anomalies, spread, departure, tally, tile, zone, ways):
    blocks = anomalies.shape[0]
    regions = math.prod(ways)
    scalars = pl.BlockSpec(memory_space=pltpu.SMEM)
    vectors = pl.BlockSpec(memory_space=pltpu.VMEM)
    return pl.pallas_call(
        functools.partial(prep_kernel, ways),
        out_shape=jax.ShapeDtypeStruct((regions, ROWS, SAMPLE_NUMBER), jnp.bfloat16),
        in_specs=[scalars] * 3 + [pl.BlockSpec(memory_space=pl.ANY)] + [vectors] * 2,
        out_specs=vectors,
        scratch_shapes=[
            pltpu.VMEM((blocks, OB, SAMPLE_NUMBER), jnp.bfloat16),
            pltpu.VMEM((regions, META, SAMPLE_NUMBER), jnp.float32),
            pltpu.SMEM((regions,), jnp.int32),
            pltpu.SemaphoreType.DMA((blocks // STEP,)),
        ],
        compiler_params=pltpu.CompilerParams(vmem_limit_bytes=24 << 20),
        cost_estimate=pl.CostEstimate(flops=0, bytes_accessed=1 << 23, transcendentals=0),
        name="build_messages",
    )(zone, tally, tile, anomalies, spread, departure)


def high_low(row):
    high = row.astype(jnp.bfloat16)
    return high, (row - high.astype(jnp.float32)).astype(jnp.bfloat16)


def gram_kernel(tag_ref, rows_ref, *refs):
    outs, (upper, corner, tag_vmem, tag_smem, tag_sem) = refs[:2], refs[2:]
    step, mem = pl.program_id(0), lax.axis_index("mem")
    sources = rows_ref.shape[0]

    @pl.when(step == 0)
    def _():
        weight = lax.broadcasted_iota(jnp.int32, tag_ref.shape, 1)
        weight = jnp.where(weight == 0, 1.0, jnp.where(weight == 1, TAGS, 0.0))
        codes = jnp.sum(tag_ref[...].astype(jnp.float32) * weight, axis=1)
        tag_vmem[...] = codes.astype(jnp.int32)
        tag_copy = pltpu.make_async_copy(tag_vmem, tag_smem, tag_sem)
        tag_copy.start()
        upper[...] = jnp.zeros_like(upper)
        corner[...] = jnp.zeros_like(corner)
        tag_copy.wait()

    place = lax.broadcasted_iota(jnp.int32, (META, OB), 0)
    for s in range(sources):
        meta = rows_ref[s, CAP * OB : ROWS, :OB].astype(jnp.float32)
        for i in range(CAP):
            code = tag_smem[step * sources + s, 0]
            tag = (code // TAGS if i else code % TAGS) - 1
            turned = ((tag // 2) ^ mem) * 2 + tag % 2
            tag = jnp.where(tag >= 0, turned, PATCH_REG)
            block = rows_ref[s, i * OB : (i + 1) * OB, :]
            flipped = block.T
            innovation = jnp.where(place == i, meta, 0.0).astype(jnp.bfloat16)
            left = jnp.concatenate([flipped[:HALF], innovation], axis=0)
            upper[tag] += jnp.dot(left, block, preferred_element_type=jnp.float32)
            corner[tag] += jnp.dot(
                flipped[HALF:], block[:, HALF:], preferred_element_type=jnp.float32
            )

    @pl.when(step == pl.num_programs(0) - 1)
    def _():
        row = lax.broadcasted_iota(jnp.int32, (HALF, HALF), 0)
        col = lax.broadcasted_iota(jnp.int32, (HALF, HALF), 1)
        for p in range(PATCH_REG):
            first, last = upper[p, :HALF, :HALF], corner[p]
            mixed = jnp.where(row >= col, first, last)
            diagonal = jnp.sum(jnp.where(row == col, last, 0.0), axis=0, keepdims=True)
            drive = jnp.sum(upper[p, HALF:, :], axis=0, keepdims=True)
            extra = jnp.concatenate([diagonal, drive[:, :HALF], drive[:, HALF:]], axis=0)
            high, low = high_low(extra)
            tail = jnp.concatenate(
                [
                    high.astype(jnp.float32),
                    low.astype(jnp.float32),
                    jnp.zeros((PACK - 2 * HALF - 6, HALF), jnp.float32),
                ],
                axis=0,
            )
            out = outs[p // 4].at[p // 2 % 2, p % 2]
            out[:HALF, :] = upper[p, :HALF, HALF:].astype(jnp.bfloat16)
            out[HALF : 2 * HALF, :] = mixed.astype(jnp.bfloat16)
            out[2 * HALF :, :] = tail.astype(jnp.bfloat16)


def partial_grams(messages):
    regions = messages.shape[0]
    sources = min(8, regions)
    pairs = jax.ShapeDtypeStruct((2, 2, PACK, HALF), jnp.bfloat16)
    return pl.pallas_call(
        gram_kernel,
        out_shape=[pairs] * 2,
        grid_spec=pl.GridSpec(
            grid=(regions // sources,),
            in_specs=[
                pl.BlockSpec((regions, META, OB), lambda i: (0, CAP * OB // META, 1)),
                pl.BlockSpec((sources, ROWS, SAMPLE_NUMBER), lambda i: (i, 0, 0)),
            ],
            out_specs=[pl.BlockSpec((2, 2, PACK, HALF), lambda i: (0, 0, 0, 0))] * 2,
            scratch_shapes=[
                pltpu.VMEM((PATCH_REG + 1, HALF + META, SAMPLE_NUMBER), jnp.float32),
                pltpu.VMEM((PATCH_REG + 1, HALF, HALF), jnp.float32),
                pltpu.VMEM((regions, OB), jnp.int32),
                pltpu.SMEM((regions, OB), jnp.int32),
                pltpu.SemaphoreType.DMA,
            ],
        ),
        compiler_params=pltpu.CompilerParams(vmem_limit_bytes=12 << 20),
        cost_estimate=pl.CostEstimate(flops=1 << 31, bytes_accessed=1 << 23, transcendentals=0),
        name="partial_grams",
    )(messages, messages)


def split(a):
    high = a.astype(jnp.bfloat16)
    return high, (a - high.astype(jnp.float32)).astype(jnp.bfloat16)


def product(a, b):
    left = jnp.concatenate([a[0], a[1], a[0]], axis=1)
    right = jnp.concatenate([b[0], b[0], b[1]], axis=0)
    return jnp.dot(left, right, preferred_element_type=jnp.float32)


def newton_kernel(a_ref, b_ref, c_ref, *refs):
    mem = lax.axis_index("mem")
    outs, (gram_ref, weight_ref) = refs[:4], refs[4:]
    row = lax.broadcasted_iota(jnp.int32, (HALF, HALF), 0)
    col = lax.broadcasted_iota(jnp.int32, (HALF, HALF), 1)
    row_full = lax.broadcasted_iota(jnp.int32, (SAMPLE_NUMBER, SAMPLE_NUMBER), 0)
    col_full = lax.broadcasted_iota(jnp.int32, (SAMPLE_NUMBER, SAMPLE_NUMBER), 1)
    identity = jnp.where(row_full == col_full, 1.0, 0.0)
    drives, frobs, roots, inverses, steps = [], [], [], [], []
    for p in range(2):
        parts = (a_ref[0, p], b_ref[0, p], c_ref[0, p], c_ref[1, p])
        total = sum(part.astype(jnp.float32) for part in parts)
        cross, mixed, tail = total[:HALF], total[HALF : 2 * HALF], total[2 * HALF :]
        extra = tail[0:3] + tail[3:6]
        turned = mixed.T
        gram_ref[p, :HALF, :HALF] = jnp.where(row >= col, mixed, turned)
        gram_ref[p, :HALF, HALF:] = cross
        gram_ref[p, HALF:, :HALF] = cross.T
        gram_ref[p, HALF:, HALF:] = jnp.where(
            row == col, extra[0:1], jnp.where(row < col, mixed, turned)
        )
        drives.append(jnp.concatenate([extra[1:2], extra[2:3]], axis=1))
        gram = gram_ref[p] + (SAMPLE_NUMBER - 1.0) * identity
        squares = jnp.sum(jnp.sum(gram * gram, axis=0, keepdims=True), axis=1, keepdims=True)
        frobs.append(jnp.sqrt(squares))
        roots.append(gram / frobs[p])
        steps.append(1.5 * identity - 0.5 * roots[p])
        inverses.append(steps[p])
    for _ in range(1, ITERS):
        step_parts = [split(step) for step in steps]
        roots = [product(split(root), step) for root, step in zip(roots, step_parts)]
        inverse_parts = [split(inverse) for inverse in inverses]
        steps = [
            1.5 * identity - 0.5 * product(inverse, split(root))
            for inverse, root in zip(inverse_parts, roots)
        ]
        inverses = [
            product(split(step), inverse) for step, inverse in zip(steps, inverse_parts)
        ]
    for p in range(2):
        inv_root = inverses[p] / jnp.sqrt(frobs[p])
        once = jnp.sum(inv_root * drives[p], axis=1, keepdims=True)
        mean_weight = jnp.sum(inv_root * once, axis=0, keepdims=True)
        weight_ref[p] = math.sqrt(SAMPLE_NUMBER - 1.0) * inv_root + mean_weight
        for e in range(4):
            goal = mem ^ e
            part = weight_ref[p, pl.ds(pl.multiple_of(goal * MEMBERS, MEMBERS), MEMBERS), :]
            low, high = part[:, :HALF], part[:, HALF:]
            low, high = jnp.where(goal >= 2, high, low), jnp.where(goal >= 2, low, high)
            for i, side in enumerate((low, high)):
                side = jnp.where(goal % 2 == 1, pltpu.roll(side, MEMBERS, 1), side)
                outs[e][p, :, i * HALF : (i + 1) * HALF] = side.astype(jnp.bfloat16)


def flipped_weights(pieces):
    piece = jax.ShapeDtypeStruct((2, MEMBERS, SAMPLE_NUMBER), jnp.bfloat16)
    return pl.pallas_call(
        newton_kernel,
        out_shape=[piece] * 4,
        scratch_shapes=[
            pltpu.VMEM((2, SAMPLE_NUMBER, SAMPLE_NUMBER), jnp.float32),
            pltpu.VMEM((2, SAMPLE_NUMBER, SAMPLE_NUMBER), jnp.float32),
        ],
        compiler_params=pltpu.CompilerParams(vmem_limit_bytes=16 << 20),
        name="weights",
    )(*pieces)


def analysis_kernel(perturb_ref, mean_ref, *refs):
    routed, out_ref = refs[:4], refs[4]
    mem = lax.axis_index("mem")
    for e in range(4):
        for i in range(2):
            p = (mem ^ e) * 2 + i
            update = jnp.dot(routed[e][i], perturb_ref[p], preferred_element_type=jnp.float32)
            out_ref[p] = (mean_ref[p] + update).astype(jnp.bfloat16)


def analysed(perturb, state_mean, routed):
    return pl.pallas_call(
        analysis_kernel,
        out_shape=jax.ShapeDtypeStruct(
            (PATCH_REG, MEMBERS, perturb.shape[2]), jnp.bfloat16
        ),
        compiler_params=pltpu.CompilerParams(vmem_limit_bytes=12 << 20),
        name="analysed",
    )(perturb, state_mean, *routed)


def swap(x, bit):
    return lax.ppermute(x, "mem", [(j, j ^ bit) for j in range(4)])


def to_owner(x, bit):
    pairs = [(m * 4 + z, (m ^ bit) * 4 + (z + ALONG[m]) % 4) for m in range(4) for z in range(4)]
    return lax.ppermute(x, ("mem", "zq"), pairs)


def per_device(prior, anomalies, spread, departure, tally, zone, tile):
    ways = {a: lax.axis_size(a) for a in ("ylo", "x", "zq", "zp")}
    in_hbm = lambda x: pltpu.with_memory_space_constraint(x, pltpu.HBM)
    far = swap(prior.reshape(-1, prior.shape[2]), 2)
    messages = build_messages(
        *(in_hbm(x) for x in (anomalies, spread, departure, tally, tile, zone[:, 0])),
        (ways["zq"], ways["ylo"] * ways["x"], ways["zp"]),
    )
    arrived = lax.all_to_all(messages, GROUP, split_axis=0, concat_axis=0, tiled=True)
    arrived, prior = lax.optimization_barrier((arrived, prior))
    near = swap(prior, 1)

    pieces = partial_grams(arrived)
    same, other = to_owner(pieces[0], 0), to_owner(pieces[1], 2)

    farther = swap(far, 1)
    far, farther = (x.reshape(prior.shape) for x in (far, farther))
    field = jnp.concatenate([prior, near, far, farther], axis=0).transpose(1, 0, 2)
    state_mean = jnp.sum(field, axis=1, keepdims=True, dtype=jnp.float32) / SAMPLE_NUMBER
    perturb = (field - state_mean).astype(jnp.bfloat16)
    same, other, state_mean, perturb = lax.optimization_barrier(
        (same, other, state_mean, perturb)
    )
    crossed = swap(jnp.stack([same[1], other[1]]), 1)
    weights = flipped_weights((same, other, crossed))
    routed = [weights[0]] + [swap(weights[e], e) for e in range(1, 4)]
    return analysed(perturb, state_mean, routed).transpose(1, 0, 2)


def solution(mesh):
    grid = Mesh(mesh.devices.reshape(4, 2, 4, 4, 2), ("mem", "ylo", "x", "zq", "zp"))
    return on_grid(grid)


def on_grid(grid):
    reg = ("ylo", "x", "zq", "zp")
    every = ("mem",) + reg
    placed = (
        P("mem", reg, None),
        P(every, None, None),
        P(every, None),
        P(every, None),
        P(every),
        P(every, None),
        P(every),
    )
    return jax.shard_map(
        per_device, mesh=grid, in_specs=placed, out_specs=P("mem", reg, None), check_vma=False
    )
```

profile of v0, /device:TPU:40, one launch (start us, length us, event | category | flops | bytes accessed | tf_op | source)
XLA Modules:
  0.0 188.2 jit_solution(18076611993086255605)
XLA Ops:
  0.0 4.4 %build_messages.1 = bf16[64,264,256]{2,1,0:T(8,128)(2,1)S(1)} custom-call(s32[64]{0:T(128)} %bitcast.14, s32[64]{0:T(128)} %tally_smem.1, s32[64]{0:T(128)} %tile_smem.1, bf16[64,128,256]{2,1,0:T(8,128)(2,1)} %anom_ref.1, f32[64,128]{1,0:T(8,128)} %spread_ref.1, f32[64,128]{1,0:T(8,128)} %depart_ref.1), custom_call_target="tpu_custom_call" | custom-call | bytes 8388608 | tf_op jit(solution)/shard_map/build_messages/pallas_call | solution.py:89
  4.4 0.0 copy-start
  4.4 3.3 %copy-done = bf16[64,264,256]{2,1,0:T(8,128)(2,1)} copy-done((bf16[64,264,256]{2,1,0:T(8,128)(2,1)}, bf16[64,264,256]{2,1,0:T(8,128)(2,1)S(1)}, u32[]{:S(2)}) %copy-start) | copy-done | bytes 8650776
  7.8 9.1 %all-to-all-start = ((bf16[64,264,256]{2,1,0:T(8,128)(2,1)}), bf16[64,264,256]{2,1,0:T(8,128)(2,1)}, u32[]{:S(2)}, u32[]{:S(2)}) async-start(bf16[64,264,256]{2,1,0:T(8,128)(2,1)} %copy-done), calls=%async_computation | async-start | bytes 17301504 | tf_op jit(solution)/shard_map/all_to_all | solution.py:315
  16.9 2.3 %collective-permute-start.3 = (bf16[512,512]{1,0:T(8,128)(2,1)S(1)}, bf16[512,512]{1,0:T(8,128)(2,1)S(1)}, u32[]{:S(2)}, u32[]{:S(2)}) collective-permute-start(bf16[512,512]{1,0:T(8,128)(2,1)S(1)} %bitcast.11), channel_id=1, source_target_pairs={{0,128},{64,192},{128,0},{192,64},{1,129},{65,193},{129,1},{193,65... | collective-permute-start | bytes 1572872 | tf_op jit(solution)/shard_map/ppermute | solution.py:299
  19.2 117.4 %collective-permute-done.3 = bf16[512,512]{1,0:T(8,128)(2,1)S(1)} collective-permute-done((bf16[512,512]{1,0:T(8,128)(2,1)S(1)}, bf16[512,512]{1,0:T(8,128)(2,1)S(1)}, u32[]{:S(2)}, u32[]{:S(2)}) %collective-permute-start.3) | collective-permute-done | bytes 524320 | tf_op jit(solution)/shard_map/ppermute | solution.py:299
  136.7 0.0 collective-permute-start.4
  136.7 0.3 all-to-all-done.tag_ref.rows_ref
  137.0 0.2 copy.12
  137.1 2.4 %collective-permute-start.2 = (bf16[64,8,512]{2,0,1:T(8,128)(2,1)S(1)}, bf16[64,8,512]{2,0,1:T(8,128)(2,1)S(1)}, u32[]{:S(2)}, u32[]{:S(2)}) collective-permute-start(bf16[64,8,512]{2,0,1:T(8,128)(2,1)S(1)} %copy.12), channel_id=1, source_target_pairs={{0,64},{64,0},{128,192},{192,128},{1,65},{65,1},{129,193},{193,129... | collective-permute-start | bytes 1572872 | tf_op jit(solution)/shard_map/ppermute | solution.py:299
  139.6 0.2 copy.13
  139.7 0.0 collective-permute-done.4
  139.7 0.2 copy.14
  139.9 10.4 %partial_grams.1 = (bf16[2,2,272,128]{3,2,1,0:T(8,128)(2,1)S(1)}, bf16[2,2,272,128]{3,2,1,0:T(8,128)(2,1)S(1)}) custom-call(bf16[64,264,256]{2,1,0:T(8,128)(2,1)} %all-to-all-done.tag_ref.rows_ref, bf16[64,264,256]{2,1,0:T(8,128)(2,1)} %all-to-all-done.tag_ref.rows_ref), custom_call_target="tpu_custom_call" | custom-call | flops 2147483648 | bytes 8388608 | tf_op jit(solution)/shard_map/partial_grams/pallas_call | solution.py:174
  150.3 0.7 collective-permute-start
  151.0 7.4 %collective-permute-start.1 = (bf16[2,2,272,128]{3,2,1,0:T(8,128)(2,1)S(1)}, bf16[2,2,272,128]{3,2,1,0:T(8,128)(2,1)S(1)}, u32[]{:S(2)}, u32[]{:S(2)}) collective-permute-start(bf16[2,2,272,128]{3,2,1,0:T(8,128)(2,1)S(1)} %get-tuple-element.19), channel_id=1, source_target_pairs={{0,128},{2,130},{4,132},{6,134},{64,196},{66,198},{68,192},{70,194... | collective-permute-start | bytes 835592 | tf_op jit(solution)/shard_map/ppermute | solution.py:304
  158.4 0.0 collective-permute-done.2
  158.4 0.3 bitcast_reduce_fusion
  158.7 0.4 fusion.perturb_ref
  159.1 0.0 collective-permute-done.a_ref
  159.1 10.7 %collective-permute-done.1.b_ref = bf16[2,2,272,128]{3,2,1,0:T(8,128)(2,1)S(1)} collective-permute-done((bf16[2,2,272,128]{3,2,1,0:T(8,128)(2,1)S(1)}, bf16[2,2,272,128]{3,2,1,0:T(8,128)(2,1)S(1)}, u32[]{:S(2)}, u32[]{:S(2)}) %collective-permute-start.1) | collective-permute-done | bytes 278560 | tf_op jit(solution)/shard_map/ppermute | solution.py:304
  169.9 0.9 collective-permute-start.5
  170.8 1.2 collective-permute-done.5.c_ref
  172.0 4.1 %weights.1 = (bf16[2,64,256]{2,1,0:T(8,128)(2,1)S(1)}, bf16[2,64,256]{2,1,0:T(8,128)(2,1)S(1)}, bf16[2,64,256]{2,1,0:T(8,128)(2,1)S(1)}, bf16[2,64,256]{2,1,0:T(8,128)(2,1)S(1)}) custom-call(bf16[2,2,272,128]{3,2,1,0:T(8,128)(2,1)S(1)} %collective-permute-done.a_ref, bf16[2,2,272,128]{3,2,1,0:T(8,128)(2,1)S(1)} %collective-permute-done.1.b_ref, ...), custom_call_target="tpu_custom_call" | custom-call | tf_op jit(solution)/shard_map/weights/pallas_call | solution.py:265
  176.1 0.5 collective-permute-start.6
  176.5 4.2 %collective-permute-start.7 = (bf16[2,64,256]{2,1,0:T(8,128)(2,1)S(1)}, bf16[2,64,256]{2,1,0:T(8,128)(2,1)S(1)}, u32[]{:S(2)}, u32[]{:S(2)}) collective-permute-start(bf16[2,64,256]{2,1,0:T(8,128)(2,1)S(1)} %get-tuple-element.27), channel_id=1, source_target_pairs={{0,128},{64,192},{128,0},{192,64},{1,129},{65,193},{129,1},{193,65... | collective-permute-start | bytes 196616 | tf_op jit(solution)/shard_map/ppermute | solution.py:299
  180.8 0.0 collective-permute-start.8
  180.8 0.0 collective-permute-done.6.refs_1_
  180.8 2.4 %collective-permute-done.7.refs_2_ = bf16[2,64,256]{2,1,0:T(8,128)(2,1)S(1)} collective-permute-done((bf16[2,64,256]{2,1,0:T(8,128)(2,1)S(1)}, bf16[2,64,256]{2,1,0:T(8,128)(2,1)S(1)}, u32[]{:S(2)}, u32[]{:S(2)}) %collective-permute-start.7) | collective-permute-done | bytes 65568 | tf_op jit(solution)/shard_map/ppermute | solution.py:299
  183.2 3.5 %collective-permute-done.8.refs_3_ = bf16[2,64,256]{2,1,0:T(8,128)(2,1)S(1)} collective-permute-done((bf16[2,64,256]{2,1,0:T(8,128)(2,1)S(1)}, bf16[2,64,256]{2,1,0:T(8,128)(2,1)S(1)}, u32[]{:S(2)}, u32[]{:S(2)}) %collective-permute-start.8) | collective-permute-done | bytes 65568 | tf_op jit(solution)/shard_map/ppermute | solution.py:299
  186.7 0.5 analysed.1
  187.1 1.1 copy.15
  (7 shorter events, 0.1 us)
Async XLA Ops:
  4.4 3.3 %copy-start = (bf16[64,264,256]{2,1,0:T(8,128)(2,1)}, bf16[64,264,256]{2,1,0:T(8,128)(2,1)S(1)}, u32[]{:S(2)}) copy-start(bf16[64,264,256]{2,1,0:T(8,128)(2,1)S(1)} %build_messages.1) | copy-start | bytes 25952260
  7.8 9.1 %copy-start.1 = (bf16[64,8,512]{2,1,0:T(8,128)(2,1)S(1)}, bf16[64,8,512]{2,1,0:T(8,128)(2,1)}, u32[]{:S(2)}) copy-start(bf16[64,8,512]{2,1,0:T(8,128)(2,1)} %param.7) | copy-start | bytes 1572868
  7.8 129.2 %all-to-all-start = ((bf16[64,264,256]{2,1,0:T(8,128)(2,1)}), bf16[64,264,256]{2,1,0:T(8,128)(2,1)}, u32[]{:S(2)}, u32[]{:S(2)}) async-start(bf16[64,264,256]{2,1,0:T(8,128)(2,1)} %copy-done), calls=%async_computation | async-start | bytes 17301504 | tf_op jit(solution)/shard_map/all_to_all | solution.py:315
  16.9 119.8 %collective-permute-start.3 = (bf16[512,512]{1,0:T(8,128)(2,1)S(1)}, bf16[512,512]{1,0:T(8,128)(2,1)S(1)}, u32[]{:S(2)}, u32[]{:S(2)}) collective-permute-start(bf16[512,512]{1,0:T(8,128)(2,1)S(1)} %bitcast.11), channel_id=1, source_target_pairs={{0,128},{64,192},{128,0},{192,64},{1,129},{65,193},{129,1},{193,65... | collective-permute-start | bytes 1572872 | tf_op jit(solution)/shard_map/ppermute | solution.py:299
  136.7 3.0 %collective-permute-start.4 = (bf16[512,512]{1,0:T(8,128)(2,1)S(1)}, bf16[512,512]{1,0:T(8,128)(2,1)S(1)}, u32[]{:S(2)}, u32[]{:S(2)}) collective-permute-start(bf16[512,512]{1,0:T(8,128)(2,1)S(1)} %collective-permute-done.3), channel_id=1, source_target_pairs={{0,64},{64,0},{128,192},{192,128},{1,65},{65,1},{129,193},{193,129... | collective-permute-start | bytes 1572872 | tf_op jit(solution)/shard_map/ppermute | solution.py:299
  137.1 21.2 %collective-permute-start.2 = (bf16[64,8,512]{2,0,1:T(8,128)(2,1)S(1)}, bf16[64,8,512]{2,0,1:T(8,128)(2,1)S(1)}, u32[]{:S(2)}, u32[]{:S(2)}) collective-permute-start(bf16[64,8,512]{2,0,1:T(8,128)(2,1)S(1)} %copy.12), channel_id=1, source_target_pairs={{0,64},{64,0},{128,192},{192,128},{1,65},{65,1},{129,193},{193,129... | collective-permute-start | bytes 1572872 | tf_op jit(solution)/shard_map/ppermute | solution.py:299
  150.3 8.9 %collective-permute-start = (bf16[2,2,272,128]{3,2,1,0:T(8,128)(2,1)S(1)}, bf16[2,2,272,128]{3,2,1,0:T(8,128)(2,1)S(1)}, u32[]{:S(2)}, u32[]{:S(2)}) collective-permute-start(bf16[2,2,272,128]{3,2,1,0:T(8,128)(2,1)S(1)} %get-tuple-element.18), channel_id=1, source_target_pairs={{0,0},{2,2},{4,4},{6,6},{64,68},{66,70},{68,64},{70,66},{128,130},... | collective-permute-start | bytes 835592 | tf_op jit(solution)/shard_map/ppermute | solution.py:304
  151.0 18.9 %collective-permute-start.1 = (bf16[2,2,272,128]{3,2,1,0:T(8,128)(2,1)S(1)}, bf16[2,2,272,128]{3,2,1,0:T(8,128)(2,1)S(1)}, u32[]{:S(2)}, u32[]{:S(2)}) collective-permute-start(bf16[2,2,272,128]{3,2,1,0:T(8,128)(2,1)S(1)} %get-tuple-element.19), channel_id=1, source_target_pairs={{0,128},{2,130},{4,132},{6,134},{64,196},{66,198},{68,192},{70,194... | collective-permute-start | bytes 835592 | tf_op jit(solution)/shard_map/ppermute | solution.py:304
  169.9 2.0 %collective-permute-start.5 = (bf16[2,2,272,128]{3,2,1,0:T(8,128)(2,1)S(1)}, bf16[2,2,272,128]{3,2,1,0:T(8,128)(2,1)S(1)}, u32[]{:S(2)}, u32[]{:S(2)}) collective-permute-start(bf16[2,2,272,128]{3,2,1,0:T(8,128)(2,1)S(1)} %pad_maximum_fusion.1), channel_id=1, source_target_pairs={{0,64},{64,0},{128,192},{192,128},{1,65},{65,1},{129,193},{193,129... | collective-permute-start | bytes 835592 | tf_op jit(solution)/shard_map/ppermute | solution.py:299
  176.1 4.7 %collective-permute-start.6 = (bf16[2,64,256]{2,1,0:T(8,128)(2,1)S(1)}, bf16[2,64,256]{2,1,0:T(8,128)(2,1)S(1)}, u32[]{:S(2)}, u32[]{:S(2)}) collective-permute-start(bf16[2,64,256]{2,1,0:T(8,128)(2,1)S(1)} %get-tuple-element.26), channel_id=1, source_target_pairs={{0,64},{64,0},{128,192},{192,128},{1,65},{65,1},{129,193},{193,129... | collective-permute-start | bytes 196616 | tf_op jit(solution)/shard_map/ppermute | solution.py:299
  176.5 6.6 %collective-permute-start.7 = (bf16[2,64,256]{2,1,0:T(8,128)(2,1)S(1)}, bf16[2,64,256]{2,1,0:T(8,128)(2,1)S(1)}, u32[]{:S(2)}, u32[]{:S(2)}) collective-permute-start(bf16[2,64,256]{2,1,0:T(8,128)(2,1)S(1)} %get-tuple-element.27), channel_id=1, source_target_pairs={{0,128},{64,192},{128,0},{192,64},{1,129},{65,193},{129,1},{193,65... | collective-permute-start | bytes 196616 | tf_op jit(solution)/shard_map/ppermute | solution.py:299
  180.8 5.9 %collective-permute-start.8 = (bf16[2,64,256]{2,1,0:T(8,128)(2,1)S(1)}, bf16[2,64,256]{2,1,0:T(8,128)(2,1)S(1)}, u32[]{:S(2)}, u32[]{:S(2)}) collective-permute-start(bf16[2,64,256]{2,1,0:T(8,128)(2,1)S(1)} %get-tuple-element.28), channel_id=1, source_target_pairs={{0,192},{64,128},{128,64},{192,0},{1,193},{65,129},{129,65},{193,1... | collective-permute-start | bytes 196616 | tf_op jit(solution)/shard_map/ppermute | solution.py:299
where the time goes:
time: 192 us; the launch traced here: 188 us
  waiting for transfers between devices  136 us (71%)
  starting transfers between devices  27.5 us (14%)
  Pallas kernels  19.4 us (10%)
  local copies, waits for them, and re-layouts  4.92 us (3%)
    ppermute x7, waiting for transfers between devices, swap(): return lax.ppermute(x, 'mem', [(j, j ^ bit) for j in range(4)])  124 us
    ppermute x2, waiting for transfers between devices, to_owner(): return lax.ppermute(x, ('mem', 'zq'), pairs)  10.7 us
    pallas_call x1, Pallas kernels, partial_grams(): pl.pallas_call(gram_kernel, out_shape=[pairs] * 2, grid_spec=pl.GridSpec(...  10.4 us
    ppermute x7, starting transfers between devices, swap(): return lax.ppermute(x, 'mem', [(j, j ^ bit) for j in range(4)])  10.3 us
    all_to_all x1, starting transfers between devices, per_device(): lax.all_to_all(messages, GROUP, split_axis=0, concat_axis=0, tiled=True)  9.14 us
    ppermute x2, starting transfers between devices, to_owner(): return lax.ppermute(x, ('mem', 'zq'), pairs)  8.08 us
    pallas_call x1, Pallas kernels, build_messages(): pl.pallas_call(functools.partial(prep_kernel, ways), out_shape=jax.ShapeD...  4.43 us
    pallas_call x1, Pallas kernels, flipped_weights(): pl.pallas_call(newton_kernel, out_shape=[piece] * 4, scratch_shapes=[pltp...  4.1 us
  transfers between devices with their start and end apart: 10, of which 6 were waited for; matrix products, arithmetic and copies ran while one was open for 1% of the time, Pallas kernels for 6%

commit v1 on v0

--- a/solution.py
+++ b/solution.py
@@ -1,4 +1,5 @@
 import functools
+import itertools
 import math
 
 import jax
@@ -32,7 +33,7 @@
 ):
     blocks = anom_ref.shape[0]
     regions = out_ref.shape[0]
-    zq_ways, plane_ways, zp_ways = ways
+    ylo_ways, x_ways, zq_ways, zp_ways = ways
     zq = lax.axis_index("zq")
 
     def load(g):
@@ -68,7 +69,10 @@
             rest = region // zp_ways
             along = (rest % zq_ways - zq + zq_ways) % zq_ways
             mem = along % 2 * 2 + along // 2
-            place = (mem * plane_ways + rest // zq_ways) * zp_ways + region % zp_ways
+            plane = (rest // zq_ways + x_ways) % (ylo_ways * x_ways)
+            zp = region % zp_ways
+            zp = jnp.where(mem == 1, zp_ways - 1 - zp, zp)
+            place = (mem * ylo_ways * x_ways + plane) * zp_ways + zp
 
             scaled = anom_buf[b].astype(jnp.float32) * weight_t[:, j : j + 1]
             start = pl.multiple_of(rank * OB, OB)
@@ -300,8 +304,14 @@
 
 
 def to_owner(x, bit):
-    pairs = [(m * 4 + z, (m ^ bit) * 4 + (z + ALONG[m]) % 4) for m in range(4) for z in range(4)]
-    return lax.ppermute(x, ("mem", "zq"), pairs)
+    axes = ("mem", "ylo", "zq", "zp")
+    sizes = [lax.axis_size(a) for a in axes]
+    pairs = []
+    for m, y, z, h in itertools.product(*(range(n) for n in sizes)):
+        goal = (m ^ bit, (y + 1) % sizes[1], (z + ALONG[m]) % sizes[2], sizes[3] - 1 - h if m == 1 else h)
+        flat = [((a * sizes[1] + b) * sizes[2] + c) * sizes[3] + d for a, b, c, d in ((m, y, z, h), goal)]
+        pairs.append(tuple(flat))
+    return lax.ppermute(x, axes, pairs)
 
 
 def per_device(prior, anomalies, spread, departure, tally, zone, tile):
@@ -310,7 +320,7 @@
     far = swap(prior.reshape(-1, prior.shape[2]), 2)
     messages = build_messages(
         *(in_hbm(x) for x in (anomalies, spread, departure, tally, tile, zone[:, 0])),
-        (ways["zq"], ways["ylo"] * ways["x"], ways["zp"]),
+        tuple(ways.values()),
     )
     arrived = lax.all_to_all(messages, GROUP, split_axis=0, concat_axis=0, tiled=True)
     arrived, prior = lax.optimization_barrier((arrived, prior))

time: 192 us -> 189 us (0.984)
  the two profiles are of different devices: /device:TPU:40 before, /device:TPU:9 now
where the time goes in v1:
time: 189 us
  waiting for transfers between devices  133 us (70%)
  starting transfers between devices  30.7 us (16%)
  Pallas kernels  19.5 us (10%)
  local copies, waits for them, and re-layouts  4.92 us (3%)
    ppermute x7, waiting for transfers between devices, swap(): return lax.ppermute(x, 'mem', [(j, j ^ bit) for j in range(4)])  121 us
    ppermute x2, starting transfers between devices, to_owner(): return lax.ppermute(x, axes, pairs)  14.1 us
    ppermute x2, waiting for transfers between devices, to_owner(): return lax.ppermute(x, axes, pairs)  11.7 us
    pallas_call x1, Pallas kernels, partial_grams(): pl.pallas_call(gram_kernel, out_shape=[pairs] * 2, grid_spec=pl.GridSpec(...  10.4 us
    all_to_all x1, starting transfers between devices, per_device(): lax.all_to_all(messages, GROUP, split_axis=0, concat_axis=0, tiled=True)  9.91 us
    ppermute x7, starting transfers between devices, swap(): return lax.ppermute(x, 'mem', [(j, j ^ bit) for j in range(4)])  6.68 us
    pallas_call x1, Pallas kernels, build_messages(): pl.pallas_call(functools.partial(prep_kernel, ways), out_shape=jax.ShapeD...  4.62 us
    pallas_call x1, Pallas kernels, flipped_weights(): pl.pallas_call(newton_kernel, out_shape=[piece] * 4, scratch_shapes=[pltp...  4.1 us
  transfers between devices with their start and end apart: 10, of which 7 were waited for; matrix products, arithmetic and copies ran while one was open for 1% of the time, Pallas kernels for 5%

profile of v1, /device:TPU:9, one launch (start us, length us, event | category | flops | bytes accessed | tf_op | source)
XLA Modules:
  0.0 188.9 jit_solution(7676385984668370212)
XLA Ops:
  0.0 4.6 %build_messages.1 = bf16[64,264,256]{2,1,0:T(8,128)(2,1)S(1)} custom-call(s32[64]{0:T(128)} %bitcast.14, s32[64]{0:T(128)} %tally_smem.1, s32[64]{0:T(128)} %tile_smem.1, bf16[64,128,256]{2,1,0:T(8,128)(2,1)} %anom_ref.1, f32[64,128]{1,0:T(8,128)} %spread_ref.1, f32[64,128]{1,0:T(8,128)} %depart_ref.1), custom_call_target="tpu_custom_call" | custom-call | bytes 8388608 | tf_op jit(solution)/shard_map/build_messages/pallas_call | solution.py:93
  4.6 3.3 %copy-done = bf16[64,264,256]{2,1,0:T(8,128)(2,1)} copy-done((bf16[64,264,256]{2,1,0:T(8,128)(2,1)}, bf16[64,264,256]{2,1,0:T(8,128)(2,1)S(1)}, u32[]{:S(2)}) %copy-start) | copy-done | bytes 8650776
  8.0 9.9 %all-to-all-start = ((bf16[64,264,256]{2,1,0:T(8,128)(2,1)}), bf16[64,264,256]{2,1,0:T(8,128)(2,1)}, u32[]{:S(2)}, u32[]{:S(2)}) async-start(bf16[64,264,256]{2,1,0:T(8,128)(2,1)} %copy-done), calls=%async_computation | async-start | bytes 17301504 | tf_op jit(solution)/shard_map/all_to_all | solution.py:325
  17.9 0.0 copy-done.1
  17.9 2.1 %collective-permute-start.3 = (bf16[512,512]{1,0:T(8,128)(2,1)S(1)}, bf16[512,512]{1,0:T(8,128)(2,1)S(1)}, u32[]{:S(2)}, u32[]{:S(2)}) collective-permute-start(bf16[512,512]{1,0:T(8,128)(2,1)S(1)} %bitcast.11), channel_id=1, source_target_pairs={{0,128},{64,192},{128,0},{192,64},{1,129},{65,193},{129,1},{193,65... | collective-permute-start | bytes 1572872 | tf_op jit(solution)/shard_map/ppermute | solution.py:303
  20.0 113.7 %collective-permute-done.3 = bf16[512,512]{1,0:T(8,128)(2,1)S(1)} collective-permute-done((bf16[512,512]{1,0:T(8,128)(2,1)S(1)}, bf16[512,512]{1,0:T(8,128)(2,1)S(1)}, u32[]{:S(2)}, u32[]{:S(2)}) %collective-permute-start.3) | collective-permute-done | bytes 524320 | tf_op jit(solution)/shard_map/ppermute | solution.py:303
  133.7 0.7 collective-permute-start.4
  134.3 0.0 all-to-all-done.tag_ref.rows_ref
  134.3 0.2 copy.12
  134.5 0.1 collective-permute-start.2
  134.6 0.2 copy.13
  134.7 1.1 collective-permute-done.4
  135.9 0.2 copy.14
  136.0 10.4 %partial_grams.1 = (bf16[2,2,272,128]{3,2,1,0:T(8,128)(2,1)S(1)}, bf16[2,2,272,128]{3,2,1,0:T(8,128)(2,1)S(1)}) custom-call(bf16[64,264,256]{2,1,0:T(8,128)(2,1)} %all-to-all-done.tag_ref.rows_ref, bf16[64,264,256]{2,1,0:T(8,128)(2,1)} %all-to-all-done.tag_ref.rows_ref), custom_call_target="tpu_custom_call" | custom-call | flops 2147483648 | bytes 8388608 | tf_op jit(solution)/shard_map/partial_grams/pallas_call | solution.py:178
  146.4 14.1 %collective-permute-start = (bf16[2,2,272,128]{3,2,1,0:T(8,128)(2,1)S(1)}, bf16[2,2,272,128]{3,2,1,0:T(8,128)(2,1)S(1)}, u32[]{:S(2)}, u32[]{:S(2)}) collective-permute-start(bf16[2,2,272,128]{3,2,1,0:T(8,128)(2,1)S(1)} %get-tuple-element.18), channel_id=1, source_target_pairs={{0,32},{1,33},{2,34},{3,35},{4,36},{5,37},{6,38},{7,39},{32,0},{33... | collective-permute-start | bytes 835592 | tf_op jit(solution)/shard_map/ppermute | solution.py:314
  160.5 0.0 collective-permute-start.1
  160.5 0.0 collective-permute-done.2
  160.5 0.3 bitcast_reduce_fusion
  160.8 0.4 fusion.perturb_ref
  161.2 6.0 %collective-permute-done.a_ref = bf16[2,2,272,128]{3,2,1,0:T(8,128)(2,1)S(1)} collective-permute-done((bf16[2,2,272,128]{3,2,1,0:T(8,128)(2,1)S(1)}, bf16[2,2,272,128]{3,2,1,0:T(8,128)(2,1)S(1)}, u32[]{:S(2)}, u32[]{:S(2)}) %collective-permute-start) | collective-permute-done | bytes 278560 | tf_op jit(solution)/shard_map/ppermute | solution.py:314
  167.2 5.7 %collective-permute-done.1.b_ref = bf16[2,2,272,128]{3,2,1,0:T(8,128)(2,1)S(1)} collective-permute-done((bf16[2,2,272,128]{3,2,1,0:T(8,128)(2,1)S(1)}, bf16[2,2,272,128]{3,2,1,0:T(8,128)(2,1)S(1)}, u32[]{:S(2)}, u32[]{:S(2)}) %collective-permute-start.1) | collective-permute-done | bytes 278560 | tf_op jit(solution)/shard_map/ppermute | solution.py:314
  173.0 0.1 collective-permute-start.5
  173.1 1.5 collective-permute-done.5.c_ref
  174.6 4.1 %weights.1 = (bf16[2,64,256]{2,1,0:T(8,128)(2,1)S(1)}, bf16[2,64,256]{2,1,0:T(8,128)(2,1)S(1)}, bf16[2,64,256]{2,1,0:T(8,128)(2,1)S(1)}, bf16[2,64,256]{2,1,0:T(8,128)(2,1)S(1)}) custom-call(bf16[2,2,272,128]{3,2,1,0:T(8,128)(2,1)S(1)} %collective-permute-done.a_ref, bf16[2,2,272,128]{3,2,1,0:T(8,128)(2,1)S(1)} %collective-permute-done.1.b_ref, ...), custom_call_target="tpu_custom_call" | custom-call | tf_op jit(solution)/shard_map/weights/pallas_call | solution.py:269
  178.7 0.2 collective-permute-start.6
  178.9 2.2 %collective-permute-start.7 = (bf16[2,64,256]{2,1,0:T(8,128)(2,1)S(1)}, bf16[2,64,256]{2,1,0:T(8,128)(2,1)S(1)}, u32[]{:S(2)}, u32[]{:S(2)}) collective-permute-start(bf16[2,64,256]{2,1,0:T(8,128)(2,1)S(1)} %get-tuple-element.27), channel_id=1, source_target_pairs={{0,128},{64,192},{128,0},{192,64},{1,129},{65,193},{129,1},{193,65... | collective-permute-start | bytes 196616 | tf_op jit(solution)/shard_map/ppermute | solution.py:303
  181.2 1.3 collective-permute-start.8
  182.5 0.0 collective-permute-done.6.refs_1_
  182.5 1.1 collective-permute-done.7.refs_2_
  183.6 3.7 %collective-permute-done.8.refs_3_ = bf16[2,64,256]{2,1,0:T(8,128)(2,1)S(1)} collective-permute-done((bf16[2,64,256]{2,1,0:T(8,128)(2,1)S(1)}, bf16[2,64,256]{2,1,0:T(8,128)(2,1)S(1)}, u32[]{:S(2)}, u32[]{:S(2)}) %collective-permute-start.8) | collective-permute-done | bytes 65568 | tf_op jit(solution)/shard_map/ppermute | solution.py:303
  187.3 0.5 analysed.1
  187.8 1.1 copy.15
  (7 shorter events, 0.1 us)
Async XLA Ops:
  4.6 3.3 %copy-start = (bf16[64,264,256]{2,1,0:T(8,128)(2,1)}, bf16[64,264,256]{2,1,0:T(8,128)(2,1)S(1)}, u32[]{:S(2)}) copy-start(bf16[64,264,256]{2,1,0:T(8,128)(2,1)S(1)} %build_messages.1) | copy-start | bytes 25952260
  8.0 9.9 %copy-start.1 = (bf16[64,8,512]{2,1,0:T(8,128)(2,1)S(1)}, bf16[64,8,512]{2,1,0:T(8,128)(2,1)}, u32[]{:S(2)}) copy-start(bf16[64,8,512]{2,1,0:T(8,128)(2,1)} %param.7) | copy-start | bytes 1572868
  8.0 126.4 %all-to-all-start = ((bf16[64,264,256]{2,1,0:T(8,128)(2,1)}), bf16[64,264,256]{2,1,0:T(8,128)(2,1)}, u32[]{:S(2)}, u32[]{:S(2)}) async-start(bf16[64,264,256]{2,1,0:T(8,128)(2,1)} %copy-done), calls=%async_computation | async-start | bytes 17301504 | tf_op jit(solution)/shard_map/all_to_all | solution.py:325
  17.9 115.8 %collective-permute-start.3 = (bf16[512,512]{1,0:T(8,128)(2,1)S(1)}, bf16[512,512]{1,0:T(8,128)(2,1)S(1)}, u32[]{:S(2)}, u32[]{:S(2)}) collective-permute-start(bf16[512,512]{1,0:T(8,128)(2,1)S(1)} %bitcast.11), channel_id=1, source_target_pairs={{0,128},{64,192},{128,0},{192,64},{1,129},{65,193},{129,1},{193,65... | collective-permute-start | bytes 1572872 | tf_op jit(solution)/shard_map/ppermute | solution.py:303
  133.7 2.2 %collective-permute-start.4 = (bf16[512,512]{1,0:T(8,128)(2,1)S(1)}, bf16[512,512]{1,0:T(8,128)(2,1)S(1)}, u32[]{:S(2)}, u32[]{:S(2)}) collective-permute-start(bf16[512,512]{1,0:T(8,128)(2,1)S(1)} %collective-permute-done.3), channel_id=1, source_target_pairs={{0,64},{64,0},{128,192},{192,128},{1,65},{65,1},{129,193},{193,129... | collective-permute-start | bytes 1572872 | tf_op jit(solution)/shard_map/ppermute | solution.py:303
  134.5 26.0 %collective-permute-start.2 = (bf16[64,8,512]{2,0,1:T(8,128)(2,1)S(1)}, bf16[64,8,512]{2,0,1:T(8,128)(2,1)S(1)}, u32[]{:S(2)}, u32[]{:S(2)}) collective-permute-start(bf16[64,8,512]{2,0,1:T(8,128)(2,1)S(1)} %copy.12), channel_id=1, source_target_pairs={{0,64},{64,0},{128,192},{192,128},{1,65},{65,1},{129,193},{193,129... | collective-permute-start | bytes 1572872 | tf_op jit(solution)/shard_map/ppermute | solution.py:303
  146.4 20.8 %collective-permute-start = (bf16[2,2,272,128]{3,2,1,0:T(8,128)(2,1)S(1)}, bf16[2,2,272,128]{3,2,1,0:T(8,128)(2,1)S(1)}, u32[]{:S(2)}, u32[]{:S(2)}) collective-permute-start(bf16[2,2,272,128]{3,2,1,0:T(8,128)(2,1)S(1)} %get-tuple-element.18), channel_id=1, source_target_pairs={{0,32},{1,33},{2,34},{3,35},{4,36},{5,37},{6,38},{7,39},{32,0},{33... | collective-permute-start | bytes 835592 | tf_op jit(solution)/shard_map/ppermute | solution.py:314
  160.5 12.4 %collective-permute-start.1 = (bf16[2,2,272,128]{3,2,1,0:T(8,128)(2,1)S(1)}, bf16[2,2,272,128]{3,2,1,0:T(8,128)(2,1)S(1)}, u32[]{:S(2)}, u32[]{:S(2)}) collective-permute-start(bf16[2,2,272,128]{3,2,1,0:T(8,128)(2,1)S(1)} %get-tuple-element.19), channel_id=1, source_target_pairs={{0,160},{1,161},{2,162},{3,163},{4,164},{5,165},{6,166},{7,167},{3... | collective-permute-start | bytes 835592 | tf_op jit(solution)/shard_map/ppermute | solution.py:314
  173.0 1.6 collective-permute-start.5
  178.7 3.7 %collective-permute-start.6 = (bf16[2,64,256]{2,1,0:T(8,128)(2,1)S(1)}, bf16[2,64,256]{2,1,0:T(8,128)(2,1)S(1)}, u32[]{:S(2)}, u32[]{:S(2)}) collective-permute-start(bf16[2,64,256]{2,1,0:T(8,128)(2,1)S(1)} %get-tuple-element.26), channel_id=1, source_target_pairs={{0,64},{64,0},{128,192},{192,128},{1,65},{65,1},{129,193},{193,129... | collective-permute-start | bytes 196616 | tf_op jit(solution)/shard_map/ppermute | solution.py:303
  178.9 4.6 %collective-permute-start.7 = (bf16[2,64,256]{2,1,0:T(8,128)(2,1)S(1)}, bf16[2,64,256]{2,1,0:T(8,128)(2,1)S(1)}, u32[]{:S(2)}, u32[]{:S(2)}) collective-permute-start(bf16[2,64,256]{2,1,0:T(8,128)(2,1)S(1)} %get-tuple-element.27), channel_id=1, source_target_pairs={{0,128},{64,192},{128,0},{192,64},{1,129},{65,193},{129,1},{193,65... | collective-permute-start | bytes 196616 | tf_op jit(solution)/shard_map/ppermute | solution.py:303
  181.2 6.1 %collective-permute-start.8 = (bf16[2,64,256]{2,1,0:T(8,128)(2,1)S(1)}, bf16[2,64,256]{2,1,0:T(8,128)(2,1)S(1)}, u32[]{:S(2)}, u32[]{:S(2)}) collective-permute-start(bf16[2,64,256]{2,1,0:T(8,128)(2,1)S(1)} %get-tuple-element.28), channel_id=1, source_target_pairs={{0,192},{64,128},{128,64},{192,0},{1,193},{65,129},{129,65},{193,1... | collective-permute-start | bytes 196616 | tf_op jit(solution)/shard_map/ppermute | solution.py:303

commit v2 on v1

--- a/solution.py
+++ b/solution.py
@@ -210,7 +210,7 @@
     return jnp.dot(left, right, preferred_element_type=jnp.float32)
 
 
-def newton_kernel(a_ref, b_ref, c_ref, *refs):
+def newton_kernel(a_ref, b_ref, c_ref, d_ref, *refs):
     mem = lax.axis_index("mem")
     outs, (gram_ref, weight_ref) = refs[:4], refs[4:]
     row = lax.broadcasted_iota(jnp.int32, (HALF, HALF), 0)
@@ -220,7 +220,7 @@
     identity = jnp.where(row_full == col_full, 1.0, 0.0)
     drives, frobs, roots, inverses, steps = [], [], [], [], []
     for p in range(2):
-        parts = (a_ref[0, p], b_ref[0, p], c_ref[0, p], c_ref[1, p])
+        parts = (a_ref[0, p], b_ref[0, p], c_ref[p], d_ref[p])
         total = sum(part.astype(jnp.float32) for part in parts)
         cross, mixed, tail = total[:HALF], total[HALF : 2 * HALF], total[2 * HALF :]
         extra = tail[0:3] + tail[3:6]
@@ -334,11 +334,9 @@
     field = jnp.concatenate([prior, near, far, farther], axis=0).transpose(1, 0, 2)
     state_mean = jnp.sum(field, axis=1, keepdims=True, dtype=jnp.float32) / SAMPLE_NUMBER
     perturb = (field - state_mean).astype(jnp.bfloat16)
-    same, other, state_mean, perturb = lax.optimization_barrier(
-        (same, other, state_mean, perturb)
-    )
-    crossed = swap(jnp.stack([same[1], other[1]]), 1)
-    weights = flipped_weights((same, other, crossed))
+    other, state_mean, perturb = lax.optimization_barrier((other, state_mean, perturb))
+    crossed = [swap(x[1], 1) for x in (same, other)]
+    weights = flipped_weights((same, other, *crossed))
     routed = [weights[0]] + [swap(weights[e], e) for e in range(1, 4)]
     return analysed(perturb, state_mean, routed).transpose(1, 0, 2)
 

time: 189 us -> 187 us (0.989)
  waiting for transfers between devices: 133 us -> 131 us
    ppermute x7 -> x8, waiting for transfers between devices: 121 us -> 120 us  [swap(): return lax.ppermute(x, 'mem', [(j, j ^ bit) for j in range(4)])]
    ppermute x7 -> x8, starting transfers between devices: 6.68 us -> 6.77 us  [swap(): return lax.ppermute(x, 'mem', [(j, j ^ bit) for j in range(4)])]
  transfers between devices with their start and end apart: 10 -> 11, of which waited for: 7 -> 6; matrix products, arithmetic and copies ran while one was open for 1% -> 1% of each run, Pallas kernels for 5% -> 6%
where the time goes in v2:
time: 187 us
  waiting for transfers between devices  131 us (70%)
  starting transfers between devices  30.8 us (16%)
  Pallas kernels  19.5 us (10%)
  local copies, waits for them, and re-layouts  4.92 us (3%)
    ppermute x8, waiting for transfers between devices, swap(): return lax.ppermute(x, 'mem', [(j, j ^ bit) for j in range(4)])  120 us
    ppermute x2, starting transfers between devices, to_owner(): return lax.ppermute(x, axes, pairs)  14.2 us
    ppermute x2, waiting for transfers between devices, to_owner(): return lax.ppermute(x, axes, pairs)  11.1 us
    pallas_call x1, Pallas kernels, partial_grams(): pl.pallas_call(gram_kernel, out_shape=[pairs] * 2, grid_spec=pl.GridSpec(...  10.3 us
    all_to_all x1, starting transfers between devices, per_device(): lax.all_to_all(messages, GROUP, split_axis=0, concat_axis=0, tiled=True)  9.91 us
    ppermute x8, starting transfers between devices, swap(): return lax.ppermute(x, 'mem', [(j, j ^ bit) for j in range(4)])  6.77 us
    pallas_call x1, Pallas kernels, build_messages(): pl.pallas_call(functools.partial(prep_kernel, ways), out_shape=jax.ShapeD...  4.62 us
    pallas_call x1, Pallas kernels, flipped_weights(): pl.pallas_call(newton_kernel, out_shape=[piece] * 4, scratch_shapes=[pltp...  4.09 us
  transfers between devices with their start and end apart: 11, of which 6 were waited for; matrix products, arithmetic and copies ran while one was open for 1% of the time, Pallas kernels for 6%

profile of v2, /device:TPU:9, one launch (start us, length us, event | category | flops | bytes accessed | tf_op | source)
XLA Modules:
  0.0 187.1 jit_solution(16726805619611869352)
XLA Ops:
  0.0 4.6 %build_messages.1 = bf16[64,264,256]{2,1,0:T(8,128)(2,1)S(1)} custom-call(s32[64]{0:T(128)} %bitcast.18, s32[64]{0:T(128)} %tally_smem.1, s32[64]{0:T(128)} %tile_smem.1, bf16[64,128,256]{2,1,0:T(8,128)(2,1)} %anom_ref.1, f32[64,128]{1,0:T(8,128)} %spread_ref.1, f32[64,128]{1,0:T(8,128)} %depart_ref.1), custom_call_target="tpu_custom_call" | custom-call | bytes 8388608 | tf_op jit(solution)/shard_map/build_messages/pallas_call | solution.py:93
  4.6 3.3 %copy-done = bf16[64,264,256]{2,1,0:T(8,128)(2,1)} copy-done((bf16[64,264,256]{2,1,0:T(8,128)(2,1)}, bf16[64,264,256]{2,1,0:T(8,128)(2,1)S(1)}, u32[]{:S(2)}) %copy-start) | copy-done | bytes 8650776
  8.0 9.9 %all-to-all-start = ((bf16[64,264,256]{2,1,0:T(8,128)(2,1)}), bf16[64,264,256]{2,1,0:T(8,128)(2,1)}, u32[]{:S(2)}, u32[]{:S(2)}) async-start(bf16[64,264,256]{2,1,0:T(8,128)(2,1)} %copy-done), calls=%async_computation | async-start | bytes 17301504 | tf_op jit(solution)/shard_map/all_to_all | solution.py:325
  17.9 2.1 %collective-permute-start.2 = (bf16[512,512]{1,0:T(8,128)(2,1)S(1)}, bf16[512,512]{1,0:T(8,128)(2,1)S(1)}, u32[]{:S(2)}, u32[]{:S(2)}) collective-permute-start(bf16[512,512]{1,0:T(8,128)(2,1)S(1)} %bitcast.15), channel_id=1, source_target_pairs={{0,128},{64,192},{128,0},{192,64},{1,129},{65,193},{129,1},{193,65... | collective-permute-start | bytes 1572872 | tf_op jit(solution)/shard_map/ppermute | solution.py:303
  20.0 113.7 %collective-permute-done.2 = bf16[512,512]{1,0:T(8,128)(2,1)S(1)} collective-permute-done((bf16[512,512]{1,0:T(8,128)(2,1)S(1)}, bf16[512,512]{1,0:T(8,128)(2,1)S(1)}, u32[]{:S(2)}, u32[]{:S(2)}) %collective-permute-start.2) | collective-permute-done | bytes 524320 | tf_op jit(solution)/shard_map/ppermute | solution.py:303
  133.7 0.7 collective-permute-start.3
  134.3 0.0 all-to-all-done.tag_ref.rows_ref
  134.3 0.2 copy.12
  134.5 0.1 collective-permute-start.1
  134.6 10.3 %partial_grams.1 = (bf16[2,2,272,128]{3,2,1,0:T(8,128)(2,1)S(1)}, bf16[2,2,272,128]{3,2,1,0:T(8,128)(2,1)S(1)}) custom-call(bf16[64,264,256]{2,1,0:T(8,128)(2,1)} %all-to-all-done.tag_ref.rows_ref, bf16[64,264,256]{2,1,0:T(8,128)(2,1)} %all-to-all-done.tag_ref.rows_ref), custom_call_target="tpu_custom_call" | custom-call | flops 2147483648 | bytes 8388608 | tf_op jit(solution)/shard_map/partial_grams/pallas_call | solution.py:178
  144.9 14.1 %collective-permute-start.4 = (bf16[2,2,272,128]{3,2,1,0:T(8,128)(2,1)S(1)}, bf16[2,2,272,128]{3,2,1,0:T(8,128)(2,1)S(1)}, u32[]{:S(2)}, u32[]{:S(2)}) collective-permute-start(bf16[2,2,272,128]{3,2,1,0:T(8,128)(2,1)S(1)} %get-tuple-element.21), channel_id=1, source_target_pairs={{0,32},{1,33},{2,34},{3,35},{4,36},{5,37},{6,38},{7,39},{32,0},{33... | collective-permute-start | bytes 835592 | tf_op jit(solution)/shard_map/ppermute | solution.py:314
  159.0 0.2 copy.13
  159.2 0.2 copy.14
  159.3 0.1 collective-permute-start
  159.4 6.3 %collective-permute-done.4.a_ref = bf16[2,2,272,128]{3,2,1,0:T(8,128)(2,1)S(1)} collective-permute-done((bf16[2,2,272,128]{3,2,1,0:T(8,128)(2,1)S(1)}, bf16[2,2,272,128]{3,2,1,0:T(8,128)(2,1)S(1)}, u32[]{:S(2)}, u32[]{:S(2)}) %collective-permute-start.4) | collective-permute-done | bytes 278560 | tf_op jit(solution)/shard_map/ppermute | solution.py:314
  165.7 0.1 collective-permute-start.5
  165.8 0.0 collective-permute-done.1
  165.8 0.3 bitcast_reduce_fusion
  166.2 0.4 fusion.perturb_ref
  166.6 4.8 %collective-permute-done.b_ref = bf16[2,2,272,128]{3,2,1,0:T(8,128)(2,1)S(1)} collective-permute-done((bf16[2,2,272,128]{3,2,1,0:T(8,128)(2,1)S(1)}, bf16[2,2,272,128]{3,2,1,0:T(8,128)(2,1)S(1)}, u32[]{:S(2)}, u32[]{:S(2)}) %collective-permute-start) | collective-permute-done | bytes 278560 | tf_op jit(solution)/shard_map/ppermute | solution.py:314
  171.5 0.1 collective-permute-start.6
  171.6 0.0 collective-permute-done.5.c_ref
  171.6 1.3 collective-permute-done.6.d_ref
  172.9 4.1 %weights.1 = (bf16[2,64,256]{2,1,0:T(8,128)(2,1)S(1)}, bf16[2,64,256]{2,1,0:T(8,128)(2,1)S(1)}, bf16[2,64,256]{2,1,0:T(8,128)(2,1)S(1)}, bf16[2,64,256]{2,1,0:T(8,128)(2,1)S(1)}) custom-call(bf16[2,2,272,128]{3,2,1,0:T(8,128)(2,1)S(1)} %collective-permute-done.4.a_ref, bf16[2,2,272,128]{3,2,1,0:T(8,128)(2,1)S(1)} %collective-permute-done.b_ref, ...), custom_call_target="tpu_custom_call" | custom-call | tf_op jit(solution)/shard_map/weights/pallas_call | solution.py:269
  177.0 0.2 collective-permute-start.7
  177.2 2.2 %collective-permute-start.8 = (bf16[2,64,256]{2,1,0:T(8,128)(2,1)S(1)}, bf16[2,64,256]{2,1,0:T(8,128)(2,1)S(1)}, u32[]{:S(2)}, u32[]{:S(2)}) collective-permute-start(bf16[2,64,256]{2,1,0:T(8,128)(2,1)S(1)} %get-tuple-element.25), channel_id=1, source_target_pairs={{0,128},{64,192},{128,0},{192,64},{1,129},{65,193},{129,1},{193,65... | collective-permute-start | bytes 196616 | tf_op jit(solution)/shard_map/ppermute | solution.py:303
  179.5 1.3 collective-permute-start.9
  180.7 0.0 collective-permute-done.7.refs_1_
  180.7 1.1 collective-permute-done.8.refs_2_
  181.9 3.7 %collective-permute-done.9.refs_3_ = bf16[2,64,256]{2,1,0:T(8,128)(2,1)S(1)} collective-permute-done((bf16[2,64,256]{2,1,0:T(8,128)(2,1)S(1)}, bf16[2,64,256]{2,1,0:T(8,128)(2,1)S(1)}, u32[]{:S(2)}, u32[]{:S(2)}) %collective-permute-start.9) | collective-permute-done | bytes 65568 | tf_op jit(solution)/shard_map/ppermute | solution.py:303
  185.6 0.5 analysed.1
  186.1 1.1 copy.15
  (8 shorter events, 0.0 us)
Async XLA Ops:
  4.6 3.3 %copy-start = (bf16[64,264,256]{2,1,0:T(8,128)(2,1)}, bf16[64,264,256]{2,1,0:T(8,128)(2,1)S(1)}, u32[]{:S(2)}) copy-start(bf16[64,264,256]{2,1,0:T(8,128)(2,1)S(1)} %build_messages.1) | copy-start | bytes 25952260
  8.0 9.9 %copy-start.1 = (bf16[64,8,512]{2,1,0:T(8,128)(2,1)S(1)}, bf16[64,8,512]{2,1,0:T(8,128)(2,1)}, u32[]{:S(2)}) copy-start(bf16[64,8,512]{2,1,0:T(8,128)(2,1)} %param.7) | copy-start | bytes 1572868
  8.0 126.4 %all-to-all-start = ((bf16[64,264,256]{2,1,0:T(8,128)(2,1)}), bf16[64,264,256]{2,1,0:T(8,128)(2,1)}, u32[]{:S(2)}, u32[]{:S(2)}) async-start(bf16[64,264,256]{2,1,0:T(8,128)(2,1)} %copy-done), calls=%async_computation | async-start | bytes 17301504 | tf_op jit(solution)/shard_map/all_to_all | solution.py:325
  17.9 115.8 %collective-permute-start.2 = (bf16[512,512]{1,0:T(8,128)(2,1)S(1)}, bf16[512,512]{1,0:T(8,128)(2,1)S(1)}, u32[]{:S(2)}, u32[]{:S(2)}) collective-permute-start(bf16[512,512]{1,0:T(8,128)(2,1)S(1)} %bitcast.15), channel_id=1, source_target_pairs={{0,128},{64,192},{128,0},{192,64},{1,129},{65,193},{129,1},{193,65... | collective-permute-start | bytes 1572872 | tf_op jit(solution)/shard_map/ppermute | solution.py:303
  133.7 25.5 %collective-permute-start.3 = (bf16[512,512]{1,0:T(8,128)(2,1)S(1)}, bf16[512,512]{1,0:T(8,128)(2,1)S(1)}, u32[]{:S(2)}, u32[]{:S(2)}) collective-permute-start(bf16[512,512]{1,0:T(8,128)(2,1)S(1)} %collective-permute-done.2), channel_id=1, source_target_pairs={{0,64},{64,0},{128,192},{192,128},{1,65},{65,1},{129,193},{193,129... | collective-permute-start | bytes 1572872 | tf_op jit(solution)/shard_map/ppermute | solution.py:303
  134.5 31.4 %collective-permute-start.1 = (bf16[64,8,512]{2,0,1:T(8,128)(2,1)S(1)}, bf16[64,8,512]{2,0,1:T(8,128)(2,1)S(1)}, u32[]{:S(2)}, u32[]{:S(2)}) collective-permute-start(bf16[64,8,512]{2,0,1:T(8,128)(2,1)S(1)} %copy.12), channel_id=1, source_target_pairs={{0,64},{64,0},{128,192},{192,128},{1,65},{65,1},{129,193},{193,129... | collective-permute-start | bytes 1572872 | tf_op jit(solution)/shard_map/ppermute | solution.py:303
  144.9 20.8 %collective-permute-start.4 = (bf16[2,2,272,128]{3,2,1,0:T(8,128)(2,1)S(1)}, bf16[2,2,272,128]{3,2,1,0:T(8,128)(2,1)S(1)}, u32[]{:S(2)}, u32[]{:S(2)}) collective-permute-start(bf16[2,2,272,128]{3,2,1,0:T(8,128)(2,1)S(1)} %get-tuple-element.21), channel_id=1, source_target_pairs={{0,32},{1,33},{2,34},{3,35},{4,36},{5,37},{6,38},{7,39},{32,0},{33... | collective-permute-start | bytes 835592 | tf_op jit(solution)/shard_map/ppermute | solution.py:314
  159.3 12.1 %collective-permute-start = (bf16[2,2,272,128]{3,2,1,0:T(8,128)(2,1)S(1)}, bf16[2,2,272,128]{3,2,1,0:T(8,128)(2,1)S(1)}, u32[]{:S(2)}, u32[]{:S(2)}) collective-permute-start(bf16[2,2,272,128]{3,2,1,0:T(8,128)(2,1)S(1)} %get-tuple-element.17), channel_id=1, source_target_pairs={{0,160},{1,161},{2,162},{3,163},{4,164},{5,165},{6,166},{7,167},{3... | collective-permute-start | bytes 835592 | tf_op jit(solution)/shard_map/ppermute | solution.py:314
  165.7 5.8 %collective-permute-start.5 = (bf16[2,272,128]{2,1,0:T(8,128)(2,1)S(1)}, bf16[2,272,128]{2,1,0:T(8,128)(2,1)S(1)}, u32[]{:S(2)}, u32[]{:S(2)}) collective-permute-start(bf16[2,272,128]{2,1,0:T(8,128)(2,1)S(1)} %slice_bitcast_fusion), channel_id=1, source_target_pairs={{0,64},{64,0},{128,192},{192,128},{1,65},{65,1},{129,193},{193,129... | collective-permute-start | bytes 417800 | tf_op jit(solution)/shard_map/ppermute | solution.py:303
  171.5 1.4 collective-permute-start.6
  177.0 3.7 %collective-permute-start.7 = (bf16[2,64,256]{2,1,0:T(8,128)(2,1)S(1)}, bf16[2,64,256]{2,1,0:T(8,128)(2,1)S(1)}, u32[]{:S(2)}, u32[]{:S(2)}) collective-permute-start(bf16[2,64,256]{2,1,0:T(8,128)(2,1)S(1)} %get-tuple-element.24), channel_id=1, source_target_pairs={{0,64},{64,0},{128,192},{192,128},{1,65},{65,1},{129,193},{193,129... | collective-permute-start | bytes 196616 | tf_op jit(solution)/shard_map/ppermute | solution.py:303
  177.2 4.6 %collective-permute-start.8 = (bf16[2,64,256]{2,1,0:T(8,128)(2,1)S(1)}, bf16[2,64,256]{2,1,0:T(8,128)(2,1)S(1)}, u32[]{:S(2)}, u32[]{:S(2)}) collective-permute-start(bf16[2,64,256]{2,1,0:T(8,128)(2,1)S(1)} %get-tuple-element.25), channel_id=1, source_target_pairs={{0,128},{64,192},{128,0},{192,64},{1,129},{65,193},{129,1},{193,65... | collective-permute-start | bytes 196616 | tf_op jit(solution)/shard_map/ppermute | solution.py:303
  179.5 6.1 %collective-permute-start.9 = (bf16[2,64,256]{2,1,0:T(8,128)(2,1)S(1)}, bf16[2,64,256]{2,1,0:T(8,128)(2,1)S(1)}, u32[]{:S(2)}, u32[]{:S(2)}) collective-permute-start(bf16[2,64,256]{2,1,0:T(8,128)(2,1)S(1)} %get-tuple-element.26), channel_id=1, source_target_pairs={{0,192},{64,128},{128,64},{192,0},{1,193},{65,129},{129,65},{193,1... | collective-permute-start | bytes 196616 | tf_op jit(solution)/shard_map/ppermute | solution.py:303
